TPU v7x, 32 devices: a whole 2x2x4 slice. The times are simulated.
32 devices in a mesh: stn: 16 (over z, y, core), pol: 2 (over x).
Axes of the slice: x: 2, y: 2, z: 4, core: 2. Of those that a mesh axis runs over, the one named last changes fastest.
Arguments:
- voltages: bfloat16 [64, 2, 2, 132992], P('stn', 'pol'), may hold values from -6 to 6, as said below
- delay_table: int32 [64], P('stn'), may hold values from 0 to 128
- channel_map: int32 [256], replicated, may hold values from 0 to 255, each once
- row_assign: int32 [32], replicated, may hold values from 0 to 31, each once
Outputs:
- bandpass: float32 [256, 128], P(('stn', 'pol'))
- lags: bfloat16 [32, 2, 256, 4, 128], P(('stn', 'pol'))
- delays: float32 [32, 4, 128], P(('stn', 'pol'))
Inputs may be any that keep to these rules, and one draw needn't show every extreme that they name: `voltages`: A station's two polarizations and its real and imaginary parts are noisy copies of common signals with station-dependent time shifts. `channel_map`: each channel appears in exactly one slot. `row_assign`: each row block appears in exactly one slot.
All inputs are finite; a program needn't handle non-finite values.
Results may differ from a plain program's by a relative error of at most 0.0059.
Values may be sent and summed in bfloat16 or wider, within the bound.
A program may use at most 128 MiB of HBM per device.

v0:
```python
import math

import jax
import jax.numpy as jnp
from jax import lax
from jax.sharding import PartitionSpec as P

CHANNELS = 256
TAPS = 8
SPECTRA = 512


def prototype():
    tap_total = TAPS * CHANNELS
    sample_index = jnp.arange(tap_total, dtype=jnp.float32)
    taper_values = 0.5 - 0.5 * jnp.cos(2.0 * math.pi * (sample_index + 0.5) / tap_total)
    offset = (sample_index - (tap_total - 1) / 2.0) / CHANNELS
    values = jnp.sin(math.pi * offset) / (math.pi * offset) * taper_values
    values = values * jnp.sqrt(CHANNELS / jnp.sum(values * values))
    return values.reshape(TAPS, CHANNELS)


def phase_parts(channels):
    cell_index = jnp.arange(CHANNELS, dtype=jnp.int32)
    phase_turns = channels[:, None] * cell_index[None, :] % CHANNELS
    phase_angle = phase_turns.astype(jnp.float32) * (2.0 * math.pi / CHANNELS)
    scale_factor = 1.0 / math.sqrt(CHANNELS)
    return (jnp.cos(phase_angle) * scale_factor, jnp.sin(phase_angle) * scale_factor)


def channel_table(channels):
    cosine, sine_part = phase_parts(channels)
    forward = jnp.stack([jnp.stack([cosine, sine_part], 1), jnp.stack([-sine_part, cosine], 1)], 0)
    return forward.astype(jnp.bfloat16)


def lag_table(channels):
    cosine, sine_part = phase_parts(channels)
    cosine = cosine.T
    sine_part = sine_part.T
    backward = jnp.stack([jnp.stack([cosine, -sine_part], 2), jnp.stack([sine_part, cosine], 2)], 0)
    return backward.astype(jnp.bfloat16)


def filter_bank(segment, window):
    framed = segment.reshape(segment.shape[:-1] + (SPECTRA + TAPS - 1, CHANNELS))
    total = jnp.zeros(segment.shape[:-1] + (SPECTRA, CHANNELS), jnp.float32)
    for tap_index in range(TAPS):
        total = (
            total
            + framed[..., tap_index : tap_index + SPECTRA, :].astype(jnp.float32)
            * window[tap_index]
        )
    return total.astype(jnp.bfloat16)


def per_device(voltages, delay_table, channel_map, row_assign):
    stn_count = lax.axis_size("stn")
    pol_count = lax.axis_size("pol")
    owner_count = stn_count * pol_count
    local_channels = CHANNELS // owner_count
    span = (SPECTRA + TAPS - 1) * CHANNELS
    window = prototype()
    position = jnp.arange(CHANNELS, dtype=jnp.int32)
    forward = channel_table(jnp.take(channel_map, position))

    def cut_segment(station_volts, start_sample):
        return lax.dynamic_slice_in_dim(station_volts, start_sample, span, 2)

    segment = jax.vmap(cut_segment)(voltages, delay_table)
    filtered = filter_bank(segment, window)
    spectra = jnp.einsum(
        "qkpc,tapsc->taqks", forward, filtered, preferred_element_type=jnp.float32
    ).astype(jnp.bfloat16)
    turned = lax.all_to_all(
        lax.all_to_all(spectra, "stn", split_axis=3, concat_axis=0, tiled=True),
        "pol",
        split_axis=3,
        concat_axis=1,
        tiled=True,
    )
    input_count = 2 * turned.shape[0]

    def correlate(channel_slot):
        channel_block = lax.dynamic_index_in_dim(turned, channel_slot, 3, keepdims=False)
        real_part = channel_block[:, :, 0].reshape(input_count, SPECTRA)
        imag_part = channel_block[:, :, 1].reshape(input_count, SPECTRA)
        stacked = jnp.concatenate([real_part, imag_part], 1)
        rotated = jnp.concatenate([-imag_part, real_part], 1)
        partner = jnp.concatenate([stacked, rotated], 0)
        product = (
            lax.dot_general(
                stacked, partner, (((1,), (1,)), ((), ())), preferred_element_type=jnp.float32
            )
            / SPECTRA
        )
        vis_real = product[:, :input_count]
        vis_imag = product[:, input_count:]
        return (jnp.stack([vis_real, vis_imag]).astype(jnp.bfloat16), jnp.diagonal(vis_real))

    visibility, bandpass = lax.map(correlate, jnp.arange(local_channels, dtype=jnp.int32))
    row_block = input_count // owner_count
    blocked = visibility.reshape(local_channels, 2, owner_count, row_block, input_count)
    block_index = jnp.arange(owner_count, dtype=jnp.int32)
    arranged = jnp.take(blocked, jnp.take(row_assign, block_index), axis=2)
    arranged = arranged.reshape(1, 1, local_channels, 2, input_count, input_count)
    regrouped = lax.all_to_all(
        lax.all_to_all(arranged, "stn", split_axis=4, concat_axis=0, tiled=True),
        "pol",
        split_axis=4,
        concat_axis=1,
        tiled=True,
    )
    gathered = regrouped.reshape(CHANNELS, 2, row_block * input_count)
    backward = lag_table(channel_map)
    lag = jnp.einsum("qlkp,kpm->qlm", backward, gathered, preferred_element_type=jnp.float32)
    power = lag[0] * lag[0] + lag[1] * lag[1]
    lag_position = jnp.where(position < CHANNELS // 2, position, position - CHANNELS).astype(
        jnp.float32
    ) / (CHANNELS // 2)
    delay = jnp.sum(power * lag_position[:, None], 0) / (jnp.sum(power, 0) + 1e-06)
    lags = lag.astype(jnp.bfloat16).reshape(1, 2, CHANNELS, row_block, input_count)
    delays = delay.reshape(1, row_block, input_count)
    return (bandpass, lags, delays)


def solution(mesh):
    in_specs = (P("stn", "pol", None, None), P("stn"), P(), P())
    out_specs = (
        P(("stn", "pol"), None),
        P(("stn", "pol"), None, None, None, None),
        P(("stn", "pol"), None, None),
    )
    return jax.shard_map(
        per_device, mesh=mesh, in_specs=in_specs, out_specs=out_specs, check_vma=False
    )
```

profile of v0, /device:TPU:1, one launch (start us, length us, event | category | flops | bytes accessed | tf_op | source)
XLA Modules:
  0.0 213.0 jit_solution(16711043971199102568)
XLA Ops:
  0.6 0.7 multiply_reduce_fusion
  1.3 2.0 gather_fusion.1
  3.3 1.3 fusion.30
  5.5 0.7 fusion.42
  6.2 17.1 %while.14 = (s32[]{:T(128)}, bf16[4,1,2,132992]{3,2,1,0:T(2,128)(2,1)}, s32[4,4]{1,0:T(4,128)S(1)}, bf16[4,1,2,132864]{3,2,1,0:T(2,128)(2,1)}, s32[]{:T(128)}) while((s32[]{:T(128)}, bf16[4,1,2,132992]{3,2,1,0:T(2,128)(2,1)}, s32[4,4]{1,0:T(4,128)S(1)}, bf16[4,1,2,132864]{3,2,1,0:T(2,128)(2,1)}, s32[]{:T(128)}) %tuple.66), condition=%wide.while_cond, body=%wide.while_body.sunk | while | flops 2 | bytes 1064561 | solution.py:68
  6.2 0.6 fusion.62
  6.8 3.7 %dynamic-slice_dynamic-update-slice_fusion.2 = bf16[4,1,2,132864]{3,2,1,0:T(2,128)(2,1)} fusion(bf16[4,1,2,132864]{3,2,1,0:T(2,128)(2,1)} %get-tuple-element.198, s32[]{:T(128)} %get-tuple-element.195, bf16[4,1,2,132992]{3,2,1,0:T(2,128)(2,1)} %get-tuple-element.201, s32[]{:T(128)} %bitcast.103, s32[]{:T(128)} %bitcast.104), kind=kLoop, calls=%fused_computation.4.clone.1 | loop fusion | bytes 1064448 | tf_op jit(solution)/shard_map/vmap()/gather
  10.5 0.6 fusion.62
  11.1 3.7 %dynamic-slice_dynamic-update-slice_fusion.2 = bf16[4,1,2,132864]{3,2,1,0:T(2,128)(2,1)} fusion(bf16[4,1,2,132864]{3,2,1,0:T(2,128)(2,1)} %get-tuple-element.198, s32[]{:T(128)} %get-tuple-element.195, bf16[4,1,2,132992]{3,2,1,0:T(2,128)(2,1)} %get-tuple-element.201, s32[]{:T(128)} %bitcast.103, s32[]{:T(128)} %bitcast.104), kind=kLoop, calls=%fused_computation.4.clone.1 | loop fusion | bytes 1064448 | tf_op jit(solution)/shard_map/vmap()/gather
  15.4 3.7 %dynamic-slice_dynamic-update-slice_fusion.2 = bf16[4,1,2,132864]{3,2,1,0:T(2,128)(2,1)} fusion(bf16[4,1,2,132864]{3,2,1,0:T(2,128)(2,1)} %get-tuple-element.198, s32[]{:T(128)} %get-tuple-element.195, bf16[4,1,2,132992]{3,2,1,0:T(2,128)(2,1)} %get-tuple-element.201, s32[]{:T(128)} %bitcast.103, s32[]{:T(128)} %bitcast.104), kind=kLoop, calls=%fused_computation.4.clone.1 | loop fusion | bytes 1064448 | tf_op jit(solution)/shard_map/vmap()/gather
  19.6 3.7 %dynamic-slice_dynamic-update-slice_fusion.2 = bf16[4,1,2,132864]{3,2,1,0:T(2,128)(2,1)} fusion(bf16[4,1,2,132864]{3,2,1,0:T(2,128)(2,1)} %get-tuple-element.198, s32[]{:T(128)} %get-tuple-element.195, bf16[4,1,2,132992]{3,2,1,0:T(2,128)(2,1)} %get-tuple-element.201, s32[]{:T(128)} %bitcast.103, s32[]{:T(128)} %bitcast.104), kind=kLoop, calls=%fused_computation.4.clone.1 | loop fusion | bytes 1064448 | tf_op jit(solution)/shard_map/vmap()/gather
  23.3 4.8 %reshape.434 = bf16[4,1,2,519,256]{4,3,2,0,1:T(8,128)(2,1)S(1)} reshape(bf16[4,1,2,132864]{3,2,1,0:T(2,128)(2,1)} %get-tuple-element.40) | data formatting | bytes 4251648 | tf_op jit(solution)/shard_map/reshape | solution.py:46
  28.2 5.6 %fusion.8 = bf16[4,1,2,256,512]{3,4,2,0,1:T(8,128)(2,1)} fusion(f32[256]{0:T(256)S(1)} %get-tuple-element.103, bf16[4,1,2,519,256]{4,3,2,0,1:T(8,128)(2,1)S(1)} %reshape.434, f32[256]{0:T(256)S(1)} %get-tuple-element.104, f32[256]{0:T(256)S(1)} %get-tuple-element.105, f32[256]{0:T(256)S(1)} %get-tuple-element.106, f32[256]{0:T(256)S(1)} %get-tuple-element.107, ...), kind=kOutput, calls=%fused_computation.25 | convolution fusion | flops 1101004800 | bytes 19406848 | tf_op jit(solution)/shard_map/qkpc,tapsc->taqks/dot_general | solution.py:72
  33.8 4.9 %copy.25 = bf16[4,1,2,256,512]{4,2,0,1,3:T(2,128)(2,1)S(1)} copy(bf16[4,1,2,256,512]{3,4,2,0,1:T(8,128)(2,1)} %fusion.8) | data formatting | bytes 4194304 | tf_op jit(solution)/shard_map/convert_element_type | solution.py:74
  38.7 54.8 %all_to_all.69 = bf16[4,1,2,256,512]{4,2,0,1,3:T(2,128)(2,1)S(1)} all-to-all(bf16[4,1,2,256,512]{4,2,0,1,3:T(2,128)(2,1)S(1)} %copy.25), channel_id=1, replica_groups=mesh['stn'=16,'pol'=2] {'stn'}, dimensions={3} | all-to-all | bytes 4194304 | tf_op jit(solution)/shard_map/all_to_all | solution.py:76
  93.6 0.7 copy.26
  94.6 3.5 %copy.28 = bf16[64,1,2,16,512]{4,2,0,1,3:T(2,128)(2,1)} copy(bf16[64,1,2,16,512]{4,3,2,0,1:T(8,128)(2,1)S(1)} %bitcast.106) | data formatting | bytes 4194304 | tf_op jit(solution)/shard_map/all_to_all | solution.py:76
  98.1 3.9 %all-to-all-start.1 = ((bf16[64,1,2,16,512]{4,2,0,1,3:T(2,128)(2,1)}), bf16[64,1,2,16,512]{4,2,0,1,3:T(2,128)(2,1)S(1)}, u32[]{:S(2)}, u32[]{:S(2)}) async-start(bf16[64,1,2,16,512]{4,2,0,1,3:T(2,128)(2,1)} %copy.28), calls=%async_computation.1 | async-start | bytes 4194304 | tf_op jit(solution)/shard_map/all_to_all | solution.py:75
  102.1 0.7 gather_fusion.2
  103.0 24.2 %all-to-all-done.1 = bf16[64,1,2,16,512]{4,2,0,1,3:T(2,128)(2,1)S(1)} async-done(((bf16[64,1,2,16,512]{4,2,0,1,3:T(2,128)(2,1)}), bf16[64,1,2,16,512]{4,2,0,1,3:T(2,128)(2,1)S(1)}, u32[]{:S(2)}, u32[]{:S(2)}) %all-to-all-start.1) | async-done | bytes 2097184 | tf_op jit(solution)/shard_map/all_to_all | solution.py:75
  127.2 2.2 %copy.41 = bf16[64,1,2,16,512]{4,3,2,0,1:T(8,128)(2,1)S(1)} copy(bf16[64,1,2,16,512]{4,2,0,1,3:T(2,128)(2,1)S(1)} %all-to-all-done.1) | data formatting | bytes 4194304 | tf_op jit(solution)/shard_map/all_to_all | solution.py:75
  129.4 1.2 copy.30
  130.6 47.9 %while.13 = (s32[]{:T(128)}, bf16[8,2,128,128]{3,2,1,0:T(8,128)(2,1)S(1)}, f32[8,128]{1,0:T(8,128)}, s32[8]{0:T(128)S(1)}, bf16[64,2,2,8,512]{4,0,3,2,1:T(8,128)(2,1)S(1)}, /*index=5*/s32[]{:T(128)}, s32[]{:T(128)}, s32[]{:T(128)}) while((s32[]{:T(128)}, bf16[8,2,128,128]{3,2,1,0:T(8,128)(2,1)S(1)}, f32[8,128]{1,0:T(8,128)}, s32[8]{0:T(128)S(1)}, ...), condition=%wide.region_2.3_spmd, body=%wide.region_1.2_spmd.sunk | while | flops 69042688 | bytes 3804815 | solution.py:101
  130.6 0.6 dynamic_slice.12
  134.1 1.2 gather_fusion
  135.3 1.3 dynamic_update_slice.12
  140.1 1.2 gather_fusion
  141.3 1.3 dynamic_update_slice.12
  146.1 1.2 gather_fusion
  147.3 1.3 dynamic_update_slice.12
  152.0 1.2 gather_fusion
  153.3 1.3 dynamic_update_slice.12
  158.0 1.2 gather_fusion
  159.3 1.3 dynamic_update_slice.12
  164.0 1.2 gather_fusion
  165.3 1.3 dynamic_update_slice.12
  170.0 1.2 gather_fusion
  171.3 1.3 dynamic_update_slice.12
  176.0 1.2 gather_fusion
  177.3 1.3 dynamic_update_slice.12
  178.9 0.6 gather_fusion.3
  179.9 18.7 %all_to_all.70 = bf16[1,1,8,2,128,128]{5,2,3,1,0,4:T(8,128)(2,1)S(1)} all-to-all(bf16[1,1,8,2,128,128]{5,2,3,1,0,4:T(8,128)(2,1)S(1)} %copy.33), channel_id=1, replica_groups=mesh['stn'=16,'pol'=2] {'stn'}, dimensions={4} | all-to-all | bytes 1048576 | tf_op jit(solution)/shard_map/all_to_all | solution.py:108
  198.6 0.9 copy.42
  199.5 3.5 %all-to-all-start.3 = ((bf16[16,1,8,2,8,128]{5,2,0,3,1,4:T(8,128)(2,1)}), bf16[16,1,8,2,8,128]{5,2,0,3,1,4:T(8,128)(2,1)S(1)}, u32[]{:S(2)}, u32[]{:S(2)}) async-start(bf16[16,1,8,2,8,128]{5,2,0,3,1,4:T(8,128)(2,1)} %bitcast.88), calls=%async_computation.3 | async-start | bytes 1048576 | tf_op jit(solution)/shard_map/all_to_all | solution.py:107
  203.0 1.2 negate_convert_fusion
  204.3 6.5 %all-to-all-done.3 = bf16[16,1,8,2,8,128]{5,2,0,3,1,4:T(8,128)(2,1)S(1)} async-done(((bf16[16,1,8,2,8,128]{5,2,0,3,1,4:T(8,128)(2,1)}), bf16[16,1,8,2,8,128]{5,2,0,3,1,4:T(8,128)(2,1)S(1)}, u32[]{:S(2)}, u32[]{:S(2)}) %all-to-all-start.3) | async-done | bytes 524320 | tf_op jit(solution)/shard_map/all_to_all | solution.py:107
  211.5 0.9 reshape.438
  212.4 0.6 fusion.39
  (152 shorter events, 14.1 us)
Async XLA Ops:
  0.6 101.4 %copy-start = (s32[32]{0:T(128)S(1)}, s32[32]{0:T(128)}, u32[]{:S(2)}) copy-start(s32[32]{0:T(128)} %param.9) | copy-start | bytes 388
  98.1 29.1 %all-to-all-start.1 = ((bf16[64,1,2,16,512]{4,2,0,1,3:T(2,128)(2,1)}), bf16[64,1,2,16,512]{4,2,0,1,3:T(2,128)(2,1)S(1)}, u32[]{:S(2)}, u32[]{:S(2)}) async-start(bf16[64,1,2,16,512]{4,2,0,1,3:T(2,128)(2,1)} %copy.28), calls=%async_computation.1 | async-start | bytes 4194304 | tf_op jit(solution)/shard_map/all_to_all | solution.py:75
  179.8 23.2 %copy-start.1 = (s32[256]{0:T(256)S(1)}, s32[256]{0:T(256)}, u32[]{:S(2)}) copy-start(s32[256]{0:T(256)} %param.8) | copy-start | bytes 3076
  199.5 11.2 %all-to-all-start.3 = ((bf16[16,1,8,2,8,128]{5,2,0,3,1,4:T(8,128)(2,1)}), bf16[16,1,8,2,8,128]{5,2,0,3,1,4:T(8,128)(2,1)S(1)}, u32[]{:S(2)}, u32[]{:S(2)}) async-start(bf16[16,1,8,2,8,128]{5,2,0,3,1,4:T(8,128)(2,1)} %bitcast.88), calls=%async_computation.3 | async-start | bytes 1048576 | tf_op jit(solution)/shard_map/all_to_all | solution.py:107
where the time goes:
time: 215 us; the launch traced here: 213 us
  blocking collectives  73.5 us (34%)
  local copies, waits for them, and re-layouts  69.6 us (32%)
  waiting for transfers between devices  30.6 us (14%)
  loops' own time  16.3 us (8%)
  matrix products  8.48 us (4%)
  starting transfers between devices  7.43 us (3%)
  other arithmetic  5.45 us (3%)
    all_to_all x1, blocking collectives, per_device(): lax.all_to_all(spectra, 'stn', split_axis=3, concat_axis=0, tiled=True)  54.8 us
    all_to_all x1, waiting for transfers between devices, per_device(): lax.all_to_all(lax.all_to_all(spectra, 'stn', split_axis=3, concat_axis=0...  24.2 us
    all_to_all x1, blocking collectives, per_device(): lax.all_to_all(arranged, 'stn', split_axis=4, concat_axis=0, tiled=True)  18.7 us
    gather x12, local copies, waits for them, and re-layouts  17.1 us
    another operation x1, loops' own time, per_device(): lax.map(correlate, jnp.arange(local_channels, dtype=jnp.int32))  16.3 us
    dynamic_update_slice x8, local copies, waits for them, and re-layouts, per_device(): lax.map(correlate, jnp.arange(local_channels, dtype=jnp.int32))  10.4 us
    gather x8, local copies, waits for them, and re-layouts, correlate(): jnp.diagonal(vis_real)  9.96 us
    all_to_all x1, waiting for transfers between devices, per_device(): lax.all_to_all(lax.all_to_all(arranged, 'stn', split_axis=4, concat_axis=...  6.45 us
  transfers between devices with their start and end apart: 2, of which 2 were waited for; matrix products, arithmetic and copies ran while one was open for 1% of the time, Pallas kernels for 0%

commit v1 on v0

v1 whole, which is shorter than its diff:
```python
import math

import jax
import jax.numpy as jnp
from jax import lax
from jax.sharding import PartitionSpec as P

CHANNELS = 256
TAPS = 8
SPECTRA = 512
AXES = ("stn", "pol")


def prototype_at(sample_index):
    tap_total = TAPS * CHANNELS
    taper_values = 0.5 - 0.5 * jnp.cos(2.0 * math.pi * (sample_index + 0.5) / tap_total)
    offset = (sample_index - (tap_total - 1) / 2.0) / CHANNELS
    return jnp.sin(math.pi * offset) / (math.pi * offset) * taper_values


def shifted_windows(delays):
    tap_total = TAPS * CHANNELS
    base = prototype_at(jnp.arange(tap_total, dtype=jnp.float32))
    scale = jnp.sqrt(CHANNELS / jnp.sum(base * base))
    index = jnp.arange((TAPS + 1) * CHANNELS, dtype=jnp.int32)[None, :] - delays[:, None]
    valid = (index >= 0) & (index < tap_total)
    values = prototype_at(index.astype(jnp.float32)) * scale
    return jnp.where(valid, values, 0.0).reshape(-1, TAPS + 1, CHANNELS)


def phase_parts(channels):
    cell_index = jnp.arange(CHANNELS, dtype=jnp.int32)
    phase_turns = channels[:, None] * cell_index[None, :] % CHANNELS
    phase_angle = phase_turns.astype(jnp.float32) * (2.0 * math.pi / CHANNELS)
    scale_factor = 1.0 / math.sqrt(CHANNELS)
    return (jnp.cos(phase_angle) * scale_factor, jnp.sin(phase_angle) * scale_factor)


def per_device(voltages, delay_table, channel_map, row_assign):
    owner_count = lax.axis_size("stn") * lax.axis_size("pol")
    stn_count = lax.axis_size("stn")
    pol_count = lax.axis_size("pol")
    local = CHANNELS // owner_count
    stations = voltages.shape[0]
    cosine, sine = phase_parts(channel_map)
    cosine = cosine.astype(jnp.bfloat16)
    sine = sine.astype(jnp.bfloat16)
    position = jnp.arange(CHANNELS, dtype=jnp.int32)

    forward = jnp.stack([jnp.stack([cosine, sine], 1), jnp.stack([-sine, cosine], 1)], 0)
    source = (position[None, :] - delay_table[:, None]) % CHANNELS
    roll = (position[None, :, None] == source[:, None, :]).astype(jnp.bfloat16)
    rolled = jnp.einsum(
        "qkpc,acd->aqkpd", forward, roll, preferred_element_type=jnp.float32
    ).astype(jnp.bfloat16)

    window = shifted_windows(delay_table)
    frames = SPECTRA + TAPS
    pad = frames * CHANNELS - voltages.shape[-1]
    framed = jnp.pad(voltages[:, 0], ((0, 0), (0, 0), (0, pad)))
    framed = framed.reshape(stations, 2, frames, CHANNELS)
    total = jnp.zeros((stations, 2, SPECTRA, CHANNELS), jnp.float32)
    for tap in range(TAPS + 1):
        total = total + framed[:, :, tap : tap + SPECTRA].astype(jnp.float32) * window[
            :, None, tap, None, :
        ]
    filtered = total.astype(jnp.bfloat16)

    spectra = jnp.einsum(
        "aqkpc,apsc->aqks", rolled, filtered, preferred_element_type=jnp.float32
    ).astype(jnp.bfloat16)
    outgoing = spectra.reshape(stations, 2, owner_count, local, SPECTRA).transpose(2, 3, 1, 0, 4)
    turned = lax.all_to_all(outgoing, AXES, split_axis=0, concat_axis=0, tiled=True)
    turned = turned.reshape(stn_count, pol_count, local, 2, stations, SPECTRA)
    inputs = owner_count * stations
    block = turned.transpose(2, 3, 0, 4, 1, 5).reshape(local, 2 * inputs, SPECTRA)

    gram = jnp.einsum("kis,kjs->kij", block, block, preferred_element_type=jnp.float32)
    vis_re = (gram[:, :inputs, :inputs] + gram[:, inputs:, inputs:]) / SPECTRA
    vis_im = (gram[:, inputs:, :inputs] - gram[:, :inputs, inputs:]) / SPECTRA
    wide = block.astype(jnp.float32)
    energy = jnp.sum(wide * wide, -1)
    bandpass = (energy[:, :inputs] + energy[:, inputs:]) / SPECTRA

    visibility = jnp.stack([vis_re, vis_im], 1).astype(jnp.bfloat16)
    rows = inputs // owner_count
    blocked = visibility.reshape(local, 2, owner_count, rows, inputs)
    arranged = jnp.take(blocked, row_assign, axis=2).transpose(2, 0, 1, 3, 4)
    gathered = lax.all_to_all(arranged, AXES, split_axis=0, concat_axis=0, tiled=True)
    gathered = gathered.reshape(CHANNELS, 2, rows * inputs)

    backward = jnp.stack(
        [jnp.stack([cosine.T, -sine.T], 2), jnp.stack([sine.T, cosine.T], 2)], 0
    )
    lag = jnp.einsum("qlkp,kpm->qlm", backward, gathered, preferred_element_type=jnp.float32)
    power = lag[0] * lag[0] + lag[1] * lag[1]
    lag_position = jnp.where(position < CHANNELS // 2, position, position - CHANNELS).astype(
        jnp.float32
    ) / (CHANNELS // 2)
    delay = jnp.sum(power * lag_position[:, None], 0) / (jnp.sum(power, 0) + 1e-06)
    lags = lag.astype(jnp.bfloat16).reshape(1, 2, CHANNELS, rows, inputs)
    return (bandpass, lags, delay.reshape(1, rows, inputs))


def solution(mesh):
    in_specs = (P("stn", "pol", None, None), P("stn"), P(), P())
    out_specs = (
        P(AXES, None),
        P(AXES, None, None, None, None),
        P(AXES, None, None),
    )
    return jax.shard_map(
        per_device, mesh=mesh, in_specs=in_specs, out_specs=out_specs, check_vma=False
    )
```

time: 215 us -> 124 us (0.58)
  blocking collectives: 73.5 us -> 0 us
  local copies, waits for them, and re-layouts: 69.6 us -> 19 us
  waiting for transfers between devices: 30.6 us -> 53.9 us
  loops' own time: 16.3 us -> 0 us
  matrix products: 8.48 us -> 20.3 us
  other arithmetic: 5.45 us -> 17.2 us
  starting transfers between devices: 7.43 us -> 11.5 us
    all_to_all x2 -> x0, blocking collectives: 73.5 us -> none  [the longest x1 54.8 us: per_device(): lax.all_to_all(spectra, 'stn', split_axis=3, concat_axis=0, tiled=True)]
    gather x24 -> x1, local copies, waits for them, and re-layouts: 30.4 us -> 1.2 us  [per_device(): arranged = jnp.take(blocked, row_assign, axis=2).transpose(2, 0, 1, 3, 4)]
    all_to_all x2, waiting for transfers between devices: 30.6 us -> 53.9 us  [the longest x1 45.1 us: per_device(): lax.all_to_all(outgoing, AXES, split_axis=0, concat_axis=0, tiled=True)]
    another operation x2 -> x0, loops' own time: 16.3 us -> none  [the longest x1 16.3 us: per_device(): lax.map(correlate, jnp.arange(local_channels, dtype=jnp.int32))]
    dot_general x9 -> x2, matrix products: 8.04 us -> 18.9 us  [the longest x1 16 us: per_device(): jnp.einsum('aqkpc,apsc->aqks', rolled, filtered, preferred_element_type=j...]
    dynamic_update_slice x8 -> x0, local copies, waits for them, and re-layouts: 10.4 us -> none  [per_device(): lax.map(correlate, jnp.arange(local_channels, dtype=jnp.int32))]
    all_to_all x6 -> x0, local copies, waits for them, and re-layouts: 7.76 us -> none  [the longest x3 4.47 us: per_device(): lax.all_to_all(spectra, 'stn', split_axis=3, concat_axis=0, tiled=True)]
    reshape x2 -> x5, local copies, waits for them, and re-layouts: 5.77 us -> 12.8 us  [the longest x1 4.1 us: per_device(): turned.transpose(2, 3, 0, 4, 1, 5).reshape(local, 2 * inputs, SPECTRA)]
  transfers between devices with their start and end apart: 2 -> 2, of which waited for: 2 -> 2; matrix products, arithmetic and copies ran while one was open for 1% -> 8% of each run, Pallas kernels for 0% -> 0%
where the time goes in v1:
time: 124 us; the launch traced here: 123 us
  waiting for transfers between devices  53.9 us (43%)
  matrix products  20.3 us (16%)
  local copies, waits for them, and re-layouts  19 us (15%)
  other arithmetic  17.2 us (14%)
  starting transfers between devices  11.5 us (9%)
  between operations  1.53 us (1%)
    all_to_all x1, waiting for transfers between devices, per_device(): lax.all_to_all(outgoing, AXES, split_axis=0, concat_axis=0, tiled=True)  45.1 us
    dot_general x1, matrix products, per_device(): jnp.einsum('aqkpc,apsc->aqks', rolled, filtered, preferred_element_type=j...  16 us
    all_to_all x1, waiting for transfers between devices, per_device(): lax.all_to_all(arranged, AXES, split_axis=0, concat_axis=0, tiled=True)  8.79 us
    all_to_all x1, starting transfers between devices, per_device(): lax.all_to_all(outgoing, AXES, split_axis=0, concat_axis=0, tiled=True)  7.09 us
    all_to_all x1, starting transfers between devices, per_device(): lax.all_to_all(arranged, AXES, split_axis=0, concat_axis=0, tiled=True)  4.41 us
    reshape x1, local copies, waits for them, and re-layouts, per_device(): turned.transpose(2, 3, 0, 4, 1, 5).reshape(local, 2 * inputs, SPECTRA)  4.1 us
    convert_element_type x2, other arithmetic, per_device(): sine = sine.astype(jnp.bfloat16)  3.78 us
    reduce_sum x1, other arithmetic, per_device(): energy = jnp.sum(wide * wide, -1)  3.73 us
  transfers between devices with their start and end apart: 2, of which 2 were waited for; matrix products, arithmetic and copies ran while one was open for 8% of the time, Pallas kernels for 0%

profile of v1, /device:TPU:1, one launch (start us, length us, event | category | flops | bytes accessed | tf_op | source)
XLA Modules:
  0.0 123.4 jit_solution(17814104276159679425)
XLA Ops:
  0.6 0.7 fusion.64
  1.3 2.0 %multiply_convert_fusion.2 = (bf16[256,1,256]{2,0,1:T(8,128)(2,1)S(1)}, bf16[256,1,256]{2,0,1:T(8,128)(2,1)S(1)}) fusion(s32[256]{0:T(256)} %param.6), kind=kLoop, calls=%fused_computation.56 | loop fusion | flops 1179648 | bytes 263168 | tf_op jit(solution)/shard_map/convert_element_type | solution.py:47
  3.3 1.7 %fusion.55 = bf16[256,1,256]{2,0,1:T(8,128)(2,1)S(1)} fusion(s32[256]{0:T(256)} %param.6), kind=kLoop, calls=%fused_computation.80 | loop fusion | flops 1245184 | bytes 132096 | tf_op jit(solution)/shard_map/neg | solution.py:50
  5.8 0.7 add_select_fusion.2
  6.5 1.2 %fusion.49 = f32[4,9,256]{2,0,1:T(4,128)S(1)} fusion(f32[]{:T(128)S(6)} %sqrt.3, s32[4]{0:T(128)} %param.5, s32[9,256]{1,0:T(8,128)S(1)} %multiply_add_fusion), kind=kLoop, calls=%fused_computation.74 | loop fusion | flops 138240 | bytes 46100 | tf_op jit(solution)/shard_map/jit(_where)/select_n | solution.py:28
  7.8 3.4 %pad.4 = bf16[4,2,133120]{2,1,0:T(2,128)(2,1)S(1)} pad(bf16[4,2,132992]{2,1,0:T(2,128)(2,1)} %bitcast.90, bf16[]{:T(256)} %constant.81.clone.1), padding=0_0x0_0x0_128 | pad | bytes 4257794 | tf_op jit(solution)/shard_map/jit(_pad)/pad | solution.py:60
  11.2 2.6 %reshape.376 = bf16[4,2,520,256]{3,2,1,0:T(8,128)(2,1)} reshape(bf16[4,2,133120]{2,1,0:T(2,128)(2,1)S(1)} %pad.4) | data formatting | bytes 4259840 | tf_op jit(solution)/shard_map/reshape | solution.py:61
  13.9 16.0 %fusion.5 = bf16[4,2,32,8,512]{4,3,2,1,0:T(8,128)(2,1)S(1)} fusion(f32[4,256]{1,0:T(4,128)S(1)} %get-tuple-element.16, bf16[4,2,520,256]{3,2,1,0:T(8,128)(2,1)} %reshape.376, f32[4,256]{1,0:T(4,128)S(1)} %get-tuple-element.17, f32[4,256]{1,0:T(4,128)S(1)} %get-tuple-element.18, f32[4,256]{1,0:T(4,128)S(1)} %get-tuple-element.19, ...), kind=kOutput, calls=%fused_computation.10 | convolution fusion | flops 1642332160 | bytes 21536768 | tf_op jit(solution)/shard_map/aqkpc,apsc->aqks/dot_general | solution.py:69
  29.8 1.7 %copy.34 = bf16[4,2,32,8,512]{4,3,1,0,2:T(8,128)(2,1)} copy(bf16[4,2,32,8,512]{4,3,2,1,0:T(8,128)(2,1)S(1)} %fusion.5) | data formatting | bytes 4194304 | tf_op jit(solution)/shard_map/reshape | solution.py:72
  31.5 0.0 copy-start.1
  31.5 0.0 copy-start
  31.5 7.1 %all-to-all-start = ((bf16[32,8,2,4,512]{4,1,2,3,0:T(8,128)(2,1)}), bf16[32,8,2,4,512]{4,1,2,3,0:T(8,128)(2,1)S(1)}, u32[]{:S(2)}, u32[]{:S(2)}) async-start(bf16[32,8,2,4,512]{4,1,2,3,0:T(8,128)(2,1)} %bitcast.88), calls=%async_computation | async-start | bytes 4194304 | tf_op jit(solution)/shard_map/all_to_all | solution.py:73
  38.6 0.0 copy-done.1
  38.6 0.0 copy-done
  38.7 1.0 fusion.56
  39.6 1.8 %multiply_convert_fusion = (bf16[256,256,1]{1,0,2:T(8,128)(2,1)}, bf16[256,256,1]{1,0,2:T(8,128)(2,1)}) fusion(s32[256]{0:T(256)S(1)} %copy-done), kind=kLoop, calls=%fused_computation.52 | loop fusion | flops 1179648 | bytes 263168 | tf_op jit(solution)/shard_map/convert_element_type | solution.py:47
  41.5 45.1 %all-to-all-done = bf16[32,8,2,4,512]{4,1,2,3,0:T(8,128)(2,1)S(1)} async-done(((bf16[32,8,2,4,512]{4,1,2,3,0:T(8,128)(2,1)}), bf16[32,8,2,4,512]{4,1,2,3,0:T(8,128)(2,1)S(1)}, u32[]{:S(2)}, u32[]{:S(2)}) %all-to-all-start) | async-done | bytes 2097184 | tf_op jit(solution)/shard_map/all_to_all | solution.py:73
  86.6 3.5 %copy.33 = bf16[16,2,8,2,4,512]{5,1,4,0,3,2:T(2,128)(2,1)} copy(bf16[16,2,8,2,4,512]{5,2,3,4,1,0:T(8,128)(2,1)S(1)} %bitcast.86) | data formatting | bytes 4194304 | tf_op jit(solution)/shard_map/reshape | solution.py:74
  90.1 4.1 %reshape.379 = bf16[8,256,512]{2,1,0:T(8,128)(2,1)} reshape(bf16[8,2,16,4,2,512]{5,4,3,2,1,0:T(2,128)(2,1)} %bitcast.89) | data formatting | bytes 4194304 | tf_op jit(solution)/shard_map/reshape | solution.py:76
  94.2 3.0 %fusion.73 = f32[8,256,256]{2,1,0:T(8,128)S(1)} fusion(bf16[8,256,512]{2,1,0:T(8,128)(2,1)} %reshape.379), kind=kOutput, calls=%fused_computation.118 | convolution fusion | flops 536870912 | bytes 4194304 | tf_op jit(solution)/shard_map/kis,kjs->kij/dot_general | solution.py:78
  97.1 0.2 fusion.17
  97.3 0.4 pad_maximum_fusion
  97.7 1.2 gather_fusion
  98.9 1.1 broadcast_select_fusion
  100.0 4.4 %all-to-all-start.1 = ((bf16[32,8,2,4,128]{4,3,1,2,0:T(4,128)(2,1)}), bf16[32,8,2,4,128]{4,3,1,2,0:T(4,128)(2,1)S(1)}, u32[]{:S(2)}, u32[]{:S(2)}) async-start(bf16[32,8,2,4,128]{4,3,1,2,0:T(4,128)(2,1)} %broadcast_select_fusion), calls=%async_computation.1 | async-start | bytes 1048576 | tf_op jit(solution)/shard_map/all_to_all | solution.py:89
  104.4 1.8 %maximum_bitcast_fusion.5 = (bf16[1,256,256,2]{2,1,3,0:T(8,128)(2,1)S(1)}, bf16[1,256,256,2]{2,1,3,0:T(8,128)(2,1)}) fusion(bf16[256,256,1]{1,0,2:T(8,128)(2,1)S(1)} %fusion.56, bf16[256,256,1]{1,0,2:T(8,128)(2,1)} %get-tuple-element.25, bf16[256,256,1]{1,0,2:T(8,128)(2,1)} %get-tuple-element.24), kind=kLoop, calls=%fused_computation.50 | loop fusion | flops 262144 | bytes 917504 | tf_op jit(solution)/shard_map/stack | solution.py:92
  106.2 3.7 %multiply_reduce_fusion = f32[8,2,16,4,2]{4,3,2,1,0:T(4,128)S(1)} fusion(bf16[16,2,8,2,4,512]{5,2,3,4,1,0:T(8,128)(2,1)S(1)} %bitcast.87), kind=kLoop, calls=%fused_computation.2 | loop fusion | flops 3143680 | bytes 2105344 | tf_op jit(solution)/shard_map/reduce_sum | solution.py:82
  109.9 0.9 copy.15
  110.8 0.7 copy.17
  111.5 8.8 %all-to-all-done.1 = bf16[32,8,2,4,128]{4,3,1,2,0:T(4,128)(2,1)S(1)} async-done(((bf16[32,8,2,4,128]{4,3,1,2,0:T(4,128)(2,1)}), bf16[32,8,2,4,128]{4,3,1,2,0:T(4,128)(2,1)S(1)}, u32[]{:S(2)}, u32[]{:S(2)}) %all-to-all-start.1) | async-done | bytes 524320 | tf_op jit(solution)/shard_map/all_to_all | solution.py:89
  120.2 1.4 %fusion.72 = (bf16[2,256,512]{2,1,0:T(8,128)(2,1)S(1)}, f32[2,256,512]{2,1,0:T(8,128)S(1)}) fusion(bf16[32,8,2,4,128]{4,3,1,2,0:T(4,128)(2,1)S(1)} %all-to-all-done.1, bf16[1,256,256,2]{2,1,3,0:T(8,128)(2,1)} %get-tuple-element.12, bf16[1,256,256,2]{2,1,3,0:T(8,128)(2,1)S(1)} %get-tuple-element.11), kind=kOutput, calls=%fused_computation.117 | convolution fusion | flops 268959744 | bytes 2621440 | tf_op jit(solution)/shard_map/qlkp,kpm->qlm/dot_general | solution.py:95
  121.6 0.9 reshape.381
  122.6 0.1 fusion.42
  122.7 0.1 fusion.26
  122.8 0.6 fusion.66
  (8 shorter events, 0.1 us)
Async XLA Ops:
  31.5 7.1 %copy-start.1 = (s32[32]{0:T(128)S(1)}, s32[32]{0:T(128)}, u32[]{:S(2)}) copy-start(s32[32]{0:T(128)} %param.7) | copy-start | bytes 388
  31.5 7.2 %copy-start = (s32[256]{0:T(256)S(1)}, s32[256]{0:T(256)}, u32[]{:S(2)}) copy-start(s32[256]{0:T(256)} %param.6) | copy-start | bytes 3076
  31.5 55.1 %all-to-all-start = ((bf16[32,8,2,4,512]{4,1,2,3,0:T(8,128)(2,1)}), bf16[32,8,2,4,512]{4,1,2,3,0:T(8,128)(2,1)S(1)}, u32[]{:S(2)}, u32[]{:S(2)}) async-start(bf16[32,8,2,4,512]{4,1,2,3,0:T(8,128)(2,1)} %bitcast.88), calls=%async_computation | async-start | bytes 4194304 | tf_op jit(solution)/shard_map/all_to_all | solution.py:73
  100.0 20.3 %all-to-all-start.1 = ((bf16[32,8,2,4,128]{4,3,1,2,0:T(4,128)(2,1)}), bf16[32,8,2,4,128]{4,3,1,2,0:T(4,128)(2,1)S(1)}, u32[]{:S(2)}, u32[]{:S(2)}) async-start(bf16[32,8,2,4,128]{4,3,1,2,0:T(4,128)(2,1)} %broadcast_select_fusion), calls=%async_computation.1 | async-start | bytes 1048576 | tf_op jit(solution)/shard_map/all_to_all | solution.py:89

commit v2 on v1

--- a/solution.py
+++ b/solution.py
@@ -9,6 +9,7 @@
 TAPS = 8
 SPECTRA = 512
 AXES = ("stn", "pol")
+CHUNKS = (256, 256)
 
 
 def prototype_at(sample_index):
@@ -28,12 +29,22 @@
     return jnp.where(valid, values, 0.0).reshape(-1, TAPS + 1, CHANNELS)
 
 
+def folded_sine(quarter):
+    x = quarter * (2.0 * math.pi / CHANNELS)
+    y = x * x
+    series = -1.0 / 39916800.0
+    for factor in (1.0 / 362880.0, -1.0 / 5040.0, 1.0 / 120.0, -1.0 / 6.0, 1.0):
+        series = series * y + factor
+    return x * series / math.sqrt(CHANNELS)
+
+
 def phase_parts(channels):
     cell_index = jnp.arange(CHANNELS, dtype=jnp.int32)
-    phase_turns = channels[:, None] * cell_index[None, :] % CHANNELS
-    phase_angle = phase_turns.astype(jnp.float32) * (2.0 * math.pi / CHANNELS)
-    scale_factor = 1.0 / math.sqrt(CHANNELS)
-    return (jnp.cos(phase_angle) * scale_factor, jnp.sin(phase_angle) * scale_factor)
+    turns = channels[:, None] * cell_index[None, :] % CHANNELS
+    half, quarter = CHANNELS // 2, CHANNELS // 4
+    cosine = jnp.abs(turns - half) - quarter
+    sine = jnp.abs((turns - quarter) % CHANNELS - half) - quarter
+    return (folded_sine(cosine.astype(jnp.float32)), folded_sine(sine.astype(jnp.float32)))
 
 
 def per_device(voltages, delay_table, channel_map, row_assign):
@@ -55,31 +66,43 @@
     ).astype(jnp.bfloat16)
 
     window = shifted_windows(delay_table)
-    frames = SPECTRA + TAPS
-    pad = frames * CHANNELS - voltages.shape[-1]
-    framed = jnp.pad(voltages[:, 0], ((0, 0), (0, 0), (0, pad)))
-    framed = framed.reshape(stations, 2, frames, CHANNELS)
-    total = jnp.zeros((stations, 2, SPECTRA, CHANNELS), jnp.float32)
-    for tap in range(TAPS + 1):
-        total = total + framed[:, :, tap : tap + SPECTRA].astype(jnp.float32) * window[
-            :, None, tap, None, :
-        ]
-    filtered = total.astype(jnp.bfloat16)
+    inputs = owner_count * stations
 
-    spectra = jnp.einsum(
-        "aqkpc,apsc->aqks", rolled, filtered, preferred_element_type=jnp.float32
-    ).astype(jnp.bfloat16)
-    outgoing = spectra.reshape(stations, 2, owner_count, local, SPECTRA).transpose(2, 3, 1, 0, 4)
-    turned = lax.all_to_all(outgoing, AXES, split_axis=0, concat_axis=0, tiled=True)
-    turned = turned.reshape(stn_count, pol_count, local, 2, stations, SPECTRA)
-    inputs = owner_count * stations
-    block = turned.transpose(2, 3, 0, 4, 1, 5).reshape(local, 2 * inputs, SPECTRA)
+    def exchange(start, count):
+        first = start * CHANNELS
+        last = min((start + count + TAPS) * CHANNELS, voltages.shape[-1])
+        framed = voltages[:, 0, :, first:last]
+        pad = (count + TAPS) * CHANNELS - (last - first)
+        framed = jnp.pad(framed, ((0, 0), (0, 0), (0, pad)))
+        framed = framed.reshape(stations, 2, count + TAPS, CHANNELS)
+        total = jnp.zeros((stations, 2, count, CHANNELS), jnp.float32)
+        for tap in range(TAPS + 1):
+            total = total + framed[:, :, tap : tap + count].astype(jnp.float32) * window[
+                :, None, tap, None, :
+            ]
+        spectra = jnp.einsum(
+            "aqkpc,apsc->aqks",
+            rolled,
+            total.astype(jnp.bfloat16),
+            preferred_element_type=jnp.float32,
+        ).astype(jnp.bfloat16)
+        outgoing = spectra.reshape(stations, 2, owner_count, local, count)
+        outgoing = outgoing.transpose(2, 3, 1, 0, 4)
+        return lax.all_to_all(outgoing, AXES, split_axis=0, concat_axis=0, tiled=True)
 
-    gram = jnp.einsum("kis,kjs->kij", block, block, preferred_element_type=jnp.float32)
+    gram = jnp.zeros((local, 2 * inputs, 2 * inputs), jnp.float32)
+    energy = jnp.zeros((local, 2 * inputs), jnp.float32)
+    start = 0
+    for count in CHUNKS:
+        turned = exchange(start, count)
+        start += count
+        turned = turned.reshape(stn_count, pol_count, local, 2, stations, count)
+        block = turned.transpose(2, 3, 0, 4, 1, 5).reshape(local, 2 * inputs, count)
+        gram = gram + jnp.einsum("kis,kjs->kij", block, block, preferred_element_type=jnp.float32)
+        wide = block.astype(jnp.float32)
+        energy = energy + jnp.sum(wide * wide, -1)
     vis_re = (gram[:, :inputs, :inputs] + gram[:, inputs:, inputs:]) / SPECTRA
     vis_im = (gram[:, inputs:, :inputs] - gram[:, :inputs, inputs:]) / SPECTRA
-    wide = block.astype(jnp.float32)
-    energy = jnp.sum(wide * wide, -1)
     bandpass = (energy[:, :inputs] + energy[:, inputs:]) / SPECTRA
 
     visibility = jnp.stack([vis_re, vis_im], 1).astype(jnp.bfloat16)

time: 124 us -> 106 us (0.85)
  waiting for transfers between devices: 53.9 us -> 45.7 us
  matrix products: 20.3 us -> 13.9 us
  other arithmetic: 17.2 us -> 13.2 us
  starting transfers between devices: 11.5 us -> 14.6 us
  local copies, waits for them, and re-layouts: 19 us -> 16.1 us
    all_to_all x1 -> x2, waiting for transfers between devices: 45.1 us -> 35.8 us  [exchange(): lax.all_to_all(outgoing, AXES, split_axis=0, concat_axis=0, tiled=True)]
    dot_general x1 -> x3, matrix products: 16 us -> 9.56 us  [the longest x2 8.8 us: exchange(): jnp.einsum('aqkpc,apsc->aqks', rolled, total.astype(jnp.bfloat16), prefer...]
    all_to_all x1 -> x2, starting transfers between devices: 7.09 us -> 10.8 us  [exchange(): lax.all_to_all(outgoing, AXES, split_axis=0, concat_axis=0, tiled=True)]
    pad x1, local copies, waits for them, and re-layouts: 3.43 us -> 0.84 us  [exchange(): framed = jnp.pad(framed, ((0, 0), (0, 0), (0, pad)))]
    convert_element_type x2, other arithmetic: 3.78 us -> 1.99 us  [per_device(): sine = sine.astype(jnp.bfloat16)]
    reshape x4 -> x8, local copies, waits for them, and re-layouts: 11.9 us -> 10.8 us  [the longest x2 4.14 us: per_device(): turned = turned.reshape(stn_count, pol_count, local, 2, stations, count)]
    dot_general x1 -> x2, matrix products: 2.95 us -> 3.89 us  [per_device(): jnp.einsum('kis,kjs->kij', block, block, preferred_element_type=jnp.float32)]
    reduce_sum x1 -> x2, other arithmetic: 3.73 us -> 4.27 us  [per_device(): energy = energy + jnp.sum(wide * wide, -1)]
  transfers between devices with their start and end apart: 2 -> 3, of which waited for: 2 -> 3; matrix products, arithmetic and copies ran while one was open for 8% -> 21% of each run, Pallas kernels for 0% -> 0%
where the time goes in v2:
time: 106 us; the launch traced here: 105 us
  waiting for transfers between devices  45.7 us (43%)
  local copies, waits for them, and re-layouts  16.1 us (15%)
  starting transfers between devices  14.6 us (14%)
  matrix products  13.9 us (13%)
  other arithmetic  13.2 us (12%)
  between operations  1.64 us (2%)
    all_to_all x2, waiting for transfers between devices, exchange(): lax.all_to_all(outgoing, AXES, split_axis=0, concat_axis=0, tiled=True)  35.8 us
    all_to_all x2, starting transfers between devices, exchange(): lax.all_to_all(outgoing, AXES, split_axis=0, concat_axis=0, tiled=True)  10.8 us
    all_to_all x1, waiting for transfers between devices, per_device(): lax.all_to_all(arranged, AXES, split_axis=0, concat_axis=0, tiled=True)  9.88 us
    dot_general x2, matrix products, exchange(): jnp.einsum('aqkpc,apsc->aqks', rolled, total.astype(jnp.bfloat16), prefer...  8.8 us
    reduce_sum x2, other arithmetic, per_device(): energy = energy + jnp.sum(wide * wide, -1)  4.27 us
    reshape x2, local copies, waits for them, and re-layouts, per_device(): turned = turned.reshape(stn_count, pol_count, local, 2, stations, count)  4.14 us
    dot_general x2, matrix products, per_device(): jnp.einsum('kis,kjs->kij', block, block, preferred_element_type=jnp.float32)  3.89 us
    all_to_all x1, starting transfers between devices, per_device(): lax.all_to_all(arranged, AXES, split_axis=0, concat_axis=0, tiled=True)  3.76 us
  transfers between devices with their start and end apart: 3, of which 3 were waited for; matrix products, arithmetic and copies ran while one was open for 21% of the time, Pallas kernels for 0%

profile of v2, /device:TPU:1, one launch (start us, length us, event | category | flops | bytes accessed | tf_op | source)
XLA Modules:
  0.0 105.1 jit_solution(8264880516705670714)
XLA Ops:
  0.6 0.0 slice-start
  0.6 1.4 %multiply_convert_fusion.2 = (bf16[256,1,256]{2,0,1:T(8,128)(2,1)S(1)}, bf16[256,1,256]{2,0,1:T(8,128)(2,1)S(1)}) fusion(s32[256]{0:T(256)} %param.6), kind=kLoop, calls=%fused_computation.93 | loop fusion | flops 4063232 | bytes 263168 | tf_op jit(solution)/shard_map/convert_element_type | solution.py:58
  2.1 1.1 %fusion.77 = bf16[256,1,256]{2,0,1:T(8,128)(2,1)S(1)} fusion(s32[256]{0:T(256)} %param.6), kind=kLoop, calls=%fused_computation.129 | loop fusion | flops 3014656 | bytes 132096 | tf_op jit(solution)/shard_map/neg | solution.py:61
  3.2 0.7 fusion.86
  3.9 0.7 add_select_fusion.4
  4.6 0.8 reshape.643
  6.1 0.0 copy-done.4
  6.1 0.6 fusion.71
  6.8 0.8 convolution_convert_fusion
  7.5 3.2 %fusion.8 = bf16[4,2,32,8,256]{4,3,2,1,0:T(8,128)(2,1)S(1)} fusion(bf16[4,256,2,256,2]{3,1,4,2,0:T(8,128)(2,1)S(1)} %convolution_convert_fusion, bf16[4,2,264,256]{3,2,1,0:T(8,128)(2,1)S(1)} %reshape.643, f32[4,256]{1,0:T(4,128)S(1)} %get-tuple-element.16, f32[4,256]{1,0:T(4,128)S(1)} %get-tuple-element.17, f32[4,256]{1,0:T(4,128)S(1)} %get-tuple-element.18, ...), kind=kOutput, calls=%fused_computation.13 | convolution fusion | flops 551550976 | bytes 12619776 | tf_op jit(solution)/shard_map/aqkpc,apsc->aqks/dot_general | solution.py:83
  10.7 0.0 copy-start
  10.8 1.1 %copy.52 = bf16[4,2,32,8,256]{4,3,1,0,2:T(8,128)(2,1)} copy(bf16[4,2,32,8,256]{4,3,2,1,0:T(8,128)(2,1)S(1)} %fusion.8) | data formatting | bytes 2097152 | tf_op jit(solution)/shard_map/reshape | solution.py:89
  11.9 7.1 %all-to-all-start = ((bf16[32,8,2,4,256]{4,1,2,3,0:T(8,128)(2,1)}), bf16[32,8,2,4,256]{4,1,2,3,0:T(8,128)(2,1)S(1)}, u32[]{:S(2)}, u32[]{:S(2)}) async-start(bf16[32,8,2,4,256]{4,1,2,3,0:T(8,128)(2,1)} %bitcast.118), calls=%async_computation | async-start | bytes 2097152 | tf_op jit(solution)/shard_map/all_to_all | solution.py:91
  19.0 0.7 slice_bitcast_fusion
  19.7 0.8 pad.4
  20.6 0.8 reshape.646
  21.3 5.6 %fusion.11 = bf16[4,2,32,8,256]{4,3,2,1,0:T(8,128)(2,1)S(1)} fusion(bf16[4,256,2,256,2]{3,1,4,2,0:T(8,128)(2,1)} %copy-done.1, bf16[4,2,264,256]{3,2,1,0:T(8,128)(2,1)S(1)} %reshape.646, f32[4,256]{1,0:T(4,128)S(1)} %get-tuple-element.16, f32[4,256]{1,0:T(4,128)S(1)} %get-tuple-element.17, f32[4,256]{1,0:T(4,128)S(1)} %get-tuple-element.18, ...), kind=kOutput, calls=%fused_computation.14 | convolution fusion | flops 551550976 | bytes 12619776 | tf_op jit(solution)/shard_map/aqkpc,apsc->aqks/dot_general | solution.py:83
  27.0 0.0 copy-start.5
  27.0 0.0 copy-start.3
  27.0 1.1 %copy.50 = bf16[4,2,32,8,256]{4,3,1,0,2:T(8,128)(2,1)} copy(bf16[4,2,32,8,256]{4,3,2,1,0:T(8,128)(2,1)S(1)} %fusion.11) | data formatting | bytes 2097152 | tf_op jit(solution)/shard_map/reshape | solution.py:89
  28.1 16.9 %all-to-all-done = bf16[32,8,2,4,256]{4,1,2,3,0:T(8,128)(2,1)S(1)} async-done(((bf16[32,8,2,4,256]{4,1,2,3,0:T(8,128)(2,1)}), bf16[32,8,2,4,256]{4,1,2,3,0:T(8,128)(2,1)S(1)}, u32[]{:S(2)}, u32[]{:S(2)}) %all-to-all-start) | async-done | bytes 1048608 | tf_op jit(solution)/shard_map/all_to_all | solution.py:91
  45.0 3.8 %all-to-all-start.1 = ((bf16[32,8,2,4,256]{4,1,2,3,0:T(8,128)(2,1)}), bf16[32,8,2,4,256]{4,1,2,3,0:T(8,128)(2,1)S(1)}, u32[]{:S(2)}, u32[]{:S(2)}) async-start(bf16[32,8,2,4,256]{4,1,2,3,0:T(8,128)(2,1)} %bitcast.111), calls=%async_computation.1 | async-start | bytes 2097152 | tf_op jit(solution)/shard_map/all_to_all | solution.py:91
  48.9 0.4 fusion.78
  49.3 0.6 multiply_convert_fusion
  49.8 0.7 maximum_bitcast_fusion.4
  50.6 2.1 %copy.51 = bf16[16,2,8,2,4,256]{5,1,4,0,3,2:T(2,128)(2,1)} copy(bf16[16,2,8,2,4,256]{5,2,3,4,1,0:T(8,128)(2,1)S(1)} %bitcast.114) | data formatting | bytes 2097152 | tf_op jit(solution)/shard_map/reshape | solution.py:99
  52.6 1.5 %reshape.649 = bf16[8,256,256]{2,1,0:T(8,128)(2,1)S(1)} reshape(bf16[8,2,16,4,2,256]{5,4,3,2,1,0:T(2,128)(2,1)} %bitcast.119) | data formatting | bytes 2097152 | tf_op jit(solution)/shard_map/reshape | solution.py:100
  54.1 1.8 %fusion.94 = f32[8,256,256]{2,1,0:T(8,128)} fusion(bf16[8,256,256]{2,1,0:T(8,128)(2,1)S(1)} %reshape.649), kind=kOutput, calls=%fused_computation.167 | convolution fusion | flops 268435456 | bytes 3145728 | tf_op jit(solution)/shard_map/kis,kjs->kij/dot_general | solution.py:101
  55.9 18.9 %all-to-all-done.1 = bf16[32,8,2,4,256]{4,1,2,3,0:T(8,128)(2,1)S(1)} async-done(((bf16[32,8,2,4,256]{4,1,2,3,0:T(8,128)(2,1)}), bf16[32,8,2,4,256]{4,1,2,3,0:T(8,128)(2,1)S(1)}, u32[]{:S(2)}, u32[]{:S(2)}) %all-to-all-start.1) | async-done | bytes 1048608 | tf_op jit(solution)/shard_map/all_to_all | solution.py:91
  74.9 2.1 %copy.49 = bf16[16,2,8,2,4,256]{5,1,4,0,3,2:T(2,128)(2,1)} copy(bf16[16,2,8,2,4,256]{5,2,3,4,1,0:T(8,128)(2,1)S(1)} %bitcast.116) | data formatting | bytes 2097152 | tf_op jit(solution)/shard_map/reshape | solution.py:99
  77.0 1.5 %reshape.650 = bf16[8,256,256]{2,1,0:T(8,128)(2,1)S(1)} reshape(bf16[8,2,16,4,2,256]{5,4,3,2,1,0:T(2,128)(2,1)} %bitcast.120) | data formatting | bytes 2097152 | tf_op jit(solution)/shard_map/reshape | solution.py:100
  78.4 2.1 %convolution_add_fusion = f32[8,256,256]{2,1,0:T(8,128)S(1)} fusion(f32[8,256,256]{2,1,0:T(8,128)} %fusion.94, bf16[8,256,256]{2,1,0:T(8,128)(2,1)S(1)} %reshape.650), kind=kOutput, calls=%fused_computation.12 | convolution fusion | flops 268959744 | bytes 5242880 | tf_op jit(solution)/shard_map/kis,kjs->kij/dot_general | solution.py:101
  80.5 0.2 fusion.22
  80.7 0.4 pad_maximum_fusion
  81.0 1.2 %gather_fusion = bf16[32,8,2,4,128]{4,3,1,2,0:T(4,128)(2,1)S(1)} fusion(bf16[8,2,32,4,128]{4,3,2,0,1:T(4,128)(2,1)S(1)} %pad_maximum_fusion, s32[1024]{0:T(1024)S(1)} %pad_clamp_fusion), kind=kCustom, calls=%fused_computation | custom fusion | bytes 1048704 | tf_op jit(solution)/shard_map/jit(_take)/gather | solution.py:111
  82.3 1.1 %broadcast_select_fusion = bf16[32,8,2,4,128]{4,3,1,2,0:T(4,128)(2,1)} fusion(bf16[32,8,2,4,128]{4,3,1,2,0:T(4,128)(2,1)S(1)} %gather_fusion, pred[32]{0:T(512)(128)(4,1)S(1)} %compare_and_fusion), kind=kLoop, calls=%fused_computation.46 | loop fusion | flops 262144 | bytes 1048608 | tf_op jit(solution)/shard_map/jit(_take)/select_n | solution.py:111
  83.4 3.8 %all-to-all-start.2 = ((bf16[32,8,2,4,128]{4,3,1,2,0:T(4,128)(2,1)}), bf16[32,8,2,4,128]{4,3,1,2,0:T(4,128)(2,1)S(1)}, u32[]{:S(2)}, u32[]{:S(2)}) async-start(bf16[32,8,2,4,128]{4,3,1,2,0:T(4,128)(2,1)} %broadcast_select_fusion), calls=%async_computation.2 | async-start | bytes 1048576 | tf_op jit(solution)/shard_map/all_to_all | solution.py:112
  87.1 2.1 %multiply_reduce_fusion.1 = f32[8,2,16,4,2]{4,3,2,1,0:T(4,128)S(1)} fusion(bf16[16,2,8,2,4,256]{5,2,3,4,1,0:T(8,128)(2,1)S(1)} %bitcast.115), kind=kLoop, calls=%fused_computation.9 | loop fusion | flops 1570816 | bytes 1056768 | tf_op jit(solution)/shard_map/reduce_sum | solution.py:103
  89.3 2.1 %multiply_reduce_fusion = f32[8,2,16,4,2]{4,3,2,1,0:T(4,128)S(1)} fusion(bf16[16,2,8,2,4,256]{5,2,3,4,1,0:T(8,128)(2,1)S(1)} %bitcast.117), kind=kLoop, calls=%fused_computation.7 | loop fusion | flops 1570816 | bytes 1056768 | tf_op jit(solution)/shard_map/reduce_sum | solution.py:103
  91.4 0.1 add.566
  91.5 0.9 copy.24
  92.4 0.7 copy.26
  93.1 9.9 %all-to-all-done.2 = bf16[32,8,2,4,128]{4,3,1,2,0:T(4,128)(2,1)S(1)} async-done(((bf16[32,8,2,4,128]{4,3,1,2,0:T(4,128)(2,1)}), bf16[32,8,2,4,128]{4,3,1,2,0:T(4,128)(2,1)S(1)}, u32[]{:S(2)}, u32[]{:S(2)}) %all-to-all-start.2) | async-done | bytes 524320 | tf_op jit(solution)/shard_map/all_to_all | solution.py:112
  103.0 0.4 fusion.93
  103.4 0.9 reshape.652
  104.3 0.1 fusion.64
  104.4 0.1 fusion.29
  104.6 0.6 fusion.88
  (17 shorter events, 0.1 us)
Async XLA Ops:
  0.6 4.0 %slice-start = ((bf16[4,1,2,132992]{3,2,1,0:T(2,128)(2,1)}), bf16[4,1,2,67584]{3,2,1,0:T(2,128)(2,1)S(1)}, s32[]{:S(2)}) async-start(bf16[4,1,2,132992]{3,2,1,0:T(2,128)(2,1)} %param.4), calls=%async_computation.3 | async-start | bytes 2162688 | tf_op jit(solution)/shard_map/slice | solution.py:74
  4.6 1.5 %copy-start.4 = (s32[4]{0:T(128)S(1)}, s32[4]{0:T(128)}, u32[]{:S(2)}) copy-start(s32[4]{0:T(128)} %param.5) | copy-start | bytes 52
  7.5 3.2 %copy-start.1 = (bf16[4,256,2,256,2]{3,1,4,2,0:T(8,128)(2,1)}, bf16[4,256,2,256,2]{3,1,4,2,0:T(8,128)(2,1)S(1)}, u32[]{:S(2)}) copy-start(bf16[4,256,2,256,2]{3,1,4,2,0:T(8,128)(2,1)S(1)} %convolution_convert_fusion) | copy-start | bytes 6291460
  10.7 8.2 %copy-start = (bf16[4,1,2,132992]{3,2,1,0:T(2,128)(2,1)S(1)}, bf16[4,1,2,132992]{3,2,1,0:T(2,128)(2,1)}, u32[]{:S(2)}) copy-start(bf16[4,1,2,132992]{3,2,1,0:T(2,128)(2,1)} %param.4) | copy-start | bytes 6383620
  11.9 33.2 %all-to-all-start = ((bf16[32,8,2,4,256]{4,1,2,3,0:T(8,128)(2,1)}), bf16[32,8,2,4,256]{4,1,2,3,0:T(8,128)(2,1)S(1)}, u32[]{:S(2)}, u32[]{:S(2)}) async-start(bf16[32,8,2,4,256]{4,1,2,3,0:T(8,128)(2,1)} %bitcast.118), calls=%async_computation | async-start | bytes 2097152 | tf_op jit(solution)/shard_map/all_to_all | solution.py:91
  27.0 21.8 %copy-start.5 = (s32[32]{0:T(128)S(1)}, s32[32]{0:T(128)}, u32[]{:S(2)}) copy-start(s32[32]{0:T(128)} %param.7) | copy-start | bytes 388
  27.0 21.9 %copy-start.3 = (s32[256]{0:T(256)S(1)}, s32[256]{0:T(256)}, u32[]{:S(2)}) copy-start(s32[256]{0:T(256)} %param.6) | copy-start | bytes 3076
  45.0 29.8 %all-to-all-start.1 = ((bf16[32,8,2,4,256]{4,1,2,3,0:T(8,128)(2,1)}), bf16[32,8,2,4,256]{4,1,2,3,0:T(8,128)(2,1)S(1)}, u32[]{:S(2)}, u32[]{:S(2)}) async-start(bf16[32,8,2,4,256]{4,1,2,3,0:T(8,128)(2,1)} %bitcast.111), calls=%async_computation.1 | async-start | bytes 2097152 | tf_op jit(solution)/shard_map/all_to_all | solution.py:91
  83.4 19.6 %all-to-all-start.2 = ((bf16[32,8,2,4,128]{4,3,1,2,0:T(4,128)(2,1)}), bf16[32,8,2,4,128]{4,3,1,2,0:T(4,128)(2,1)S(1)}, u32[]{:S(2)}, u32[]{:S(2)}) async-start(bf16[32,8,2,4,128]{4,3,1,2,0:T(4,128)(2,1)} %broadcast_select_fusion), calls=%async_computation.2 | async-start | bytes 1048576 | tf_op jit(solution)/shard_map/all_to_all | solution.py:112
  89.3 13.7 %copy-start.2 = (bf16[1,256,256,2]{2,1,3,0:T(8,128)(2,1)S(1)}, bf16[1,256,256,2]{2,1,3,0:T(8,128)(2,1)}, u32[]{:S(2)}) copy-start(bf16[1,256,256,2]{2,1,3,0:T(8,128)(2,1)} %get-tuple-element.12) | copy-start | bytes 786436

commit v3 on v2

--- a/solution.py
+++ b/solution.py
@@ -3,6 +3,8 @@
 import jax
 import jax.numpy as jnp
 from jax import lax
+from jax.experimental import pallas as pl
+from jax.experimental.pallas import tpu as pltpu
 from jax.sharding import PartitionSpec as P
 
 CHANNELS = 256
@@ -45,6 +47,194 @@
     cosine = jnp.abs(turns - half) - quarter
     sine = jnp.abs((turns - quarter) % CHANNELS - half) - quarter
     return (folded_sine(cosine.astype(jnp.float32)), folded_sine(sine.astype(jnp.float32)))
+
+
+def row_table(channels):
+    rows = lax.broadcasted_iota(jnp.int32, (2 * CHANNELS, 2 * CHANNELS), 0)
+    cells = lax.broadcasted_iota(jnp.int32, (2 * CHANNELS, 2 * CHANNELS), 1)
+    quarter = CHANNELS // 4
+    turns = jnp.repeat(channels, 2)[:, None] * (cells % CHANNELS)
+    turns = (turns + quarter * (rows % 2 - cells // CHANNELS)) % CHANNELS
+    folded = jnp.abs(turns - CHANNELS // 2) - quarter
+    return folded_sine(folded.astype(jnp.float32)).astype(jnp.bfloat16)
+
+
+def each(count, body):
+    def step(index, carry):
+        body(index)
+        return carry
+
+    lax.fori_loop(0, count, step, 0)
+
+
+def exchange_kernel(
+    filtered, framed, window, table, shift, regroup, gram, stage, send, recv, block, send_sem, recv_sem
+):
+    pol_count = lax.axis_size("pol")
+    owners = lax.axis_size("stn") * pol_count
+    me = lax.axis_index("stn") * pol_count + lax.axis_index("pol")
+    stations = filtered.shape[0]
+    count = filtered.shape[2]
+
+    def place(index):
+        return (index // pol_count, index % pol_count)
+
+    barrier = pltpu.get_barrier_semaphore()
+
+    def greet(offset):
+        pl.semaphore_signal(
+            barrier,
+            inc=1,
+            device_id=place((me + 1 + offset) % owners),
+            device_id_type=pl.DeviceIdType.MESH,
+        )
+
+    each(owners - 1, greet)
+
+    def remote(half, source, target):
+        return pltpu.make_async_remote_copy(
+            src_ref=send.at[half, target],
+            dst_ref=recv.at[half, source],
+            send_sem=send_sem.at[half, target],
+            recv_sem=recv_sem.at[half, source],
+            device_id=place(target),
+            device_id_type=pl.DeviceIdType.MESH,
+        )
+
+    def own(half):
+        return pltpu.make_async_copy(
+            send.at[half, me], recv.at[half, me], recv_sem.at[half, me]
+        )
+
+    def turn(rows, moves):
+        return jnp.dot(rows, moves, preferred_element_type=jnp.float32).astype(jnp.bfloat16)
+
+    def transform(half, values):
+        def station(a):
+            product = lax.dot_general(
+                turn(table[:, :CHANNELS], shift[a]),
+                values[a, 0],
+                (((1,), (1,)), ((), ())),
+                preferred_element_type=jnp.float32,
+            ) + lax.dot_general(
+                turn(table[:, CHANNELS:], shift[a]),
+                values[a, 1],
+                (((1,), (1,)), ((), ())),
+                preferred_element_type=jnp.float32,
+            )
+            send[half, :, a] = product.astype(jnp.bfloat16).reshape(owners, -1, count)
+
+        each(stations, station)
+
+    def deliver(half):
+        own(half).start()
+
+        def start(step):
+            offset = step // 4 + (owners // 4) * ((step + 2) % 4)
+
+            @pl.when(offset != 0)
+            def _():
+                remote(half, me, (me + offset) % owners).start()
+
+        each(owners, start)
+
+    def filter_rest():
+        def part(index):
+            a = index // 2
+            p = index % 2
+            total = jnp.zeros((count, CHANNELS), jnp.float32)
+            wide = framed[a, p].astype(jnp.float32)
+            for tap in range(TAPS + 1):
+                total = total + wide[tap : tap + count] * window[a, tap : tap + 1]
+            stage[a, p] = total.astype(jnp.bfloat16)
+
+        each(stations * 2, part)
+
+    def correlate(half):
+        group = 256 // (stations * block.shape[0])
+
+        own(half).wait()
+
+        def arrive(offset):
+            remote(half, (me + 1 + offset) % owners, me).wait_recv()
+
+        each(owners - 1, arrive)
+
+        def gather(g):
+            rows = recv[half, pl.ds(g * group, group)].reshape(256, count)
+            moved = jnp.dot(regroup[...], rows, preferred_element_type=jnp.float32)
+            width = group * stations
+            block[:, pl.ds(pl.multiple_of(g * width, width), width)] = moved.astype(
+                jnp.bfloat16
+            ).reshape(-1, width, count)
+
+        each(owners // group, gather)
+
+        def channel(k):
+            rows = block[pl.ds(2 * k, 2)].reshape(-1, count)
+            product = lax.dot_general(
+                rows, rows, (((1,), (1,)), ((), ())), preferred_element_type=jnp.float32
+            )
+            if half == 0:
+                gram[k] = product
+            else:
+                gram[k] = gram[k] + product
+
+        each(gram.shape[0], channel)
+
+    transform(0, filtered)
+    pl.semaphore_wait(barrier, owners - 1)
+    deliver(0)
+    filter_rest()
+    transform(1, stage)
+    deliver(1)
+    correlate(0)
+    correlate(1)
+
+    def sent(offset):
+        target = (me + 1 + offset) % owners
+        for half in range(2):
+            pltpu.make_async_remote_copy(
+                src_ref=send.at[half, target],
+                dst_ref=recv.at[half, me],
+                send_sem=send_sem.at[half, target],
+                recv_sem=recv_sem.at[half, me],
+                device_id=place(target),
+                device_id_type=pl.DeviceIdType.MESH,
+            ).wait_send()
+
+    each(owners - 1, sent)
+
+
+def kernel_gram(filtered, framed, window, table, shift, owners, local):
+    stations = filtered.shape[0]
+    count = filtered.shape[2]
+    rows = 2 * local
+    inputs = owners * stations
+    group = 256 // (stations * rows)
+    index = jnp.arange(256, dtype=jnp.int32)
+    r, il = index // (group * stations), index % (group * stations)
+    stn, rest = il // (2 * stations), il % (2 * stations)
+    source = ((stn * 2 + rest % 2) * stations + rest // 2) * rows + r
+    regroup = (index[None, :] == source[:, None]).astype(jnp.bfloat16)
+    vmem = pl.BlockSpec(memory_space=pltpu.VMEM)
+    return pl.pallas_call(
+        exchange_kernel,
+        out_shape=jax.ShapeDtypeStruct((local, 2 * inputs, 2 * inputs), jnp.float32),
+        in_specs=[vmem] * 6,
+        out_specs=vmem,
+        scratch_shapes=[
+            pltpu.VMEM((stations, 2, count, CHANNELS), jnp.bfloat16),
+            pltpu.VMEM((2, owners, stations, rows, count), jnp.bfloat16),
+            pltpu.VMEM((2, owners, stations, rows, count), jnp.bfloat16),
+            pltpu.VMEM((rows, inputs, count), jnp.bfloat16),
+            pltpu.SemaphoreType.DMA((2, owners)),
+            pltpu.SemaphoreType.DMA((2, owners)),
+        ],
+        compiler_params=pltpu.CompilerParams(
+            collective_id=0, has_side_effects=True, vmem_limit_bytes=48 * 1024 * 1024
+        ),
+    )(filtered, framed, window, table, shift, regroup)
 
 
 def per_device(voltages, delay_table, channel_map, row_assign):
@@ -68,39 +258,60 @@
     window = shifted_windows(delay_table)
     inputs = owner_count * stations
 
-    def exchange(start, count):
+    def frame(start, count):
         first = start * CHANNELS
         last = min((start + count + TAPS) * CHANNELS, voltages.shape[-1])
         framed = voltages[:, 0, :, first:last]
         pad = (count + TAPS) * CHANNELS - (last - first)
         framed = jnp.pad(framed, ((0, 0), (0, 0), (0, pad)))
-        framed = framed.reshape(stations, 2, count + TAPS, CHANNELS)
+        return framed.reshape(stations, 2, count + TAPS, CHANNELS)
+
+    def filter_frames(framed, count):
         total = jnp.zeros((stations, 2, count, CHANNELS), jnp.float32)
         for tap in range(TAPS + 1):
             total = total + framed[:, :, tap : tap + count].astype(jnp.float32) * window[
                 :, None, tap, None, :
             ]
+        return total.astype(jnp.bfloat16)
+
+    def exchange(start, count):
+        filtered = filter_frames(frame(start, count), count)
         spectra = jnp.einsum(
             "aqkpc,apsc->aqks",
             rolled,
-            total.astype(jnp.bfloat16),
+            filtered,
             preferred_element_type=jnp.float32,
         ).astype(jnp.bfloat16)
         outgoing = spectra.reshape(stations, 2, owner_count, local, count)
         outgoing = outgoing.transpose(2, 3, 1, 0, 4)
         return lax.all_to_all(outgoing, AXES, split_axis=0, concat_axis=0, tiled=True)
 
-    gram = jnp.zeros((local, 2 * inputs, 2 * inputs), jnp.float32)
-    energy = jnp.zeros((local, 2 * inputs), jnp.float32)
-    start = 0
-    for count in CHUNKS:
-        turned = exchange(start, count)
-        start += count
-        turned = turned.reshape(stn_count, pol_count, local, 2, stations, count)
-        block = turned.transpose(2, 3, 0, 4, 1, 5).reshape(local, 2 * inputs, count)
-        gram = gram + jnp.einsum("kis,kjs->kij", block, block, preferred_element_type=jnp.float32)
-        wide = block.astype(jnp.float32)
-        energy = energy + jnp.sum(wide * wide, -1)
+    if local * stations * 2 == 64 and pol_count == 2:
+        count = SPECTRA // 2
+        table = row_table(channel_map)
+        gram = kernel_gram(
+            filter_frames(frame(0, count), count),
+            frame(count, count),
+            window,
+            table,
+            roll,
+            owner_count,
+            local,
+        )
+        same = jnp.arange(2 * inputs)[:, None] == jnp.arange(2 * inputs)[None, :]
+        energy = jnp.sum(jnp.where(same, gram, 0.0), -1)
+    else:
+        gram = jnp.zeros((local, 2 * inputs, 2 * inputs), jnp.float32)
+        energy = jnp.zeros((local, 2 * inputs), jnp.float32)
+        start = 0
+        for count in CHUNKS:
+            turned = exchange(start, count)
+            start += count
+            turned = turned.reshape(stn_count, pol_count, local, 2, stations, count)
+            block = turned.transpose(2, 3, 0, 4, 1, 5).reshape(local, 2 * inputs, count)
+            gram = gram + jnp.einsum("kis,kjs->kij", block, block, preferred_element_type=jnp.float32)
+            wide = block.astype(jnp.float32)
+            energy = energy + jnp.sum(wide * wide, -1)
     vis_re = (gram[:, :inputs, :inputs] + gram[:, inputs:, inputs:]) / SPECTRA
     vis_im = (gram[:, inputs:, :inputs] - gram[:, :inputs, inputs:]) / SPECTRA
     bandpass = (energy[:, :inputs] + energy[:, inputs:]) / SPECTRA

time: 106 us -> 100 us (0.943)
  Pallas kernels: 0 us -> 58.2 us
  waiting for transfers between devices: 45.7 us -> 13.8 us
  matrix products: 13.9 us -> 0.44 us
  starting transfers between devices: 14.6 us -> 3.96 us
  local copies, waits for them, and re-layouts: 16.1 us -> 11.3 us
  other arithmetic: 13.2 us -> 10.4 us
    pallas_call x0 -> x1, Pallas kernels: none -> 58.2 us  [kernel_gram(): pl.pallas_call(exchange_kernel, out_shape=jax.ShapeDtypeStruct((local, 2...]
    all_to_all x2 -> x0, waiting for transfers between devices: 35.8 us -> none  [exchange(): lax.all_to_all(outgoing, AXES, split_axis=0, concat_axis=0, tiled=True)]
    dot_general x5 -> x0, matrix products: 13.4 us -> none  [the longest x2 8.8 us: exchange(): jnp.einsum('aqkpc,apsc->aqks', rolled, total.astype(jnp.bfloat16), prefer...]
    all_to_all x2 -> x0, starting transfers between devices: 10.8 us -> none  [exchange(): lax.all_to_all(outgoing, AXES, split_axis=0, concat_axis=0, tiled=True)]
    reshape x8 -> x2, local copies, waits for them, and re-layouts: 10.8 us -> 3.22 us  [frame(): return framed.reshape(stations, 2, count + TAPS, CHANNELS)]
    convert_element_type x0 -> x4, other arithmetic: none -> 4.57 us  [the longest x1 2.36 us: filter_frames(): return total.astype(jnp.bfloat16)]
    all_to_all x1, waiting for transfers between devices: 9.88 us -> 13.8 us  [per_device(): lax.all_to_all(arranged, AXES, split_axis=0, concat_axis=0, tiled=True)]
    reduce_sum x2 -> x1, other arithmetic: 4.27 us -> 0.36 us  [per_device(): energy = jnp.sum(jnp.where(same, gram, 0.0), -1)]
  transfers between devices with their start and end apart: 3 -> 1, of which waited for: 3 -> 1; matrix products, arithmetic and copies ran while one was open for 21% -> 2% of each run, Pallas kernels for 0% -> 0%
where the time goes in v3:
time: 100 us; the launch traced here: 99.7 us
  Pallas kernels  58.2 us (58%)
  waiting for transfers between devices  13.8 us (14%)
  local copies, waits for them, and re-layouts  11.3 us (11%)
  other arithmetic  10.4 us (10%)
  starting transfers between devices  3.96 us (4%)
  between operations  1.65 us (2%)
    pallas_call x1, Pallas kernels, kernel_gram(): pl.pallas_call(exchange_kernel, out_shape=jax.ShapeDtypeStruct((local, 2...  58.2 us
    all_to_all x1, waiting for transfers between devices, per_device(): lax.all_to_all(arranged, AXES, split_axis=0, concat_axis=0, tiled=True)  13.8 us
    all_to_all x1, starting transfers between devices, per_device(): lax.all_to_all(arranged, AXES, split_axis=0, concat_axis=0, tiled=True)  3.96 us
    reshape x2, local copies, waits for them, and re-layouts, frame(): return framed.reshape(stations, 2, count + TAPS, CHANNELS)  3.22 us
    pad x1, local copies, waits for them, and re-layouts, frame(): framed = jnp.pad(framed, ((0, 0), (0, 0), (0, pad)))  3.06 us
    convert_element_type x1, other arithmetic, filter_frames(): return total.astype(jnp.bfloat16)  2.36 us
  transfers between devices with their start and end apart: 1, of which 1 were waited for; matrix products, arithmetic and copies ran while one was open for 2% of the time, Pallas kernels for 0%

profile of v3, /device:TPU:1, one launch (start us, length us, event | category | flops | bytes accessed | tf_op | source)
XLA Modules:
  0.0 99.7 jit_solution(1603636055919837998)
XLA Ops:
  0.6 0.0 copy-start
  0.7 0.7 fusion.54
  1.4 0.0 copy-start.3
  1.4 0.0 copy-start.2
  1.4 0.0 slice-start
  1.4 0.8 copy-done
  2.2 0.0 copy-start.1
  2.2 1.7 %slice_bitcast_fusion = bf16[4,2,67456]{2,1,0:T(2,128)(2,1)} fusion(bf16[4,1,2,132992]{3,2,1,0:T(2,128)(2,1)S(1)} %copy-done), kind=kLoop, calls=%fused_computation.7 | loop fusion | bytes 2158592 | tf_op jit(solution)/shard_map/squeeze | solution.py:264
  4.0 0.0 copy-done.3
  4.8 0.0 copy-done.2
  4.8 0.1 add_select_fusion.3
  4.9 0.5 fusion.40.window
  5.4 0.0 slice-done
  5.4 0.8 reshape.452
  6.2 0.0 copy-done.1
  6.2 0.1 broadcast_in_dim.42
  6.3 0.1 mul.493
  6.5 3.1 %pad.4 = bf16[4,2,67584]{2,1,0:T(2,128)(2,1)} pad(bf16[4,2,67456]{2,1,0:T(2,128)(2,1)} %slice_bitcast_fusion, bf16[]{:T(256)} %constant.210.clone.1), padding=0_0x0_0x0_128 | pad | bytes 2160642 | tf_op jit(solution)/shard_map/jit(_pad)/pad | solution.py:266
  9.5 2.5 %reshape.453.framed = bf16[4,2,264,256]{3,2,1,0:T(8,128)(2,1)S(1)} reshape(bf16[4,2,67584]{2,1,0:T(2,128)(2,1)} %pad.4) | data formatting | bytes 2162688 | tf_op jit(solution)/shard_map/reshape | solution.py:267
  12.0 0.2 fusion.9.shift
  12.1 0.1 fusion.33.regroup
  12.3 2.4 %add_convert_fusion.filtered = bf16[4,2,256,256]{3,2,1,0:T(8,128)(2,1)S(1)} fusion(bf16[4,2,264,256]{3,2,1,0:T(8,128)(2,1)S(1)} %reshape.452, f32[4,256]{1,0:T(4,128)S(1)} %get-tuple-element.20, f32[4,256]{1,0:T(4,128)S(1)} %get-tuple-element.21, f32[4,256]{1,0:T(4,128)S(1)} %get-tuple-element.22, f32[4,256]{1,0:T(4,128)S(1)} %get-tuple-element.23, ...), kind=kLoop, calls=%fused_computation.2 | loop fusion | flops 14155776 | bytes 10522624 | tf_op jit(solution)/shard_map/convert_element_type | solution.py:275
  14.7 2.0 %multiply_convert_fusion.table = bf16[512,512]{1,0:T(8,128)(2,1)S(1)} fusion(s32[512]{0:T(512)S(1)} %get-tuple-element.28, s32[512]{0:T(512)S(1)} %get-tuple-element.33, s32[512]{0:T(512)S(1)} %get-tuple-element.29, s32[512]{0:T(512)S(1)} %get-tuple-element.30, s32[512]{0:T(512)S(1)} %get-tuple-element.31, s32[512]{0:T(512)S(1)} %get-tuple-element.32, ...), kind=kLoop, calls=%fused_computation.15 | loop fusion | flops 9699328 | bytes 540160 | tf_op jit(solution)/shard_map/convert_element_type | solution.py:59
  16.6 58.2 %shard_map.67 = f32[8,256,256]{2,1,0:T(8,128)S(1)} custom-call(bf16[4,2,256,256]{3,2,1,0:T(8,128)(2,1)S(1)} %add_convert_fusion.filtered, bf16[4,2,264,256]{3,2,1,0:T(8,128)(2,1)S(1)} %reshape.453.framed, f32[4,9,256]{2,1,0:T(8,128)S(1)} %fusion.40.window, bf16[512,512]{1,0:T(8,128)(2,1)S(1)} %multiply_convert_fusion.table, ...), custom_call_target="tpu_custom_call" | custom-call | tf_op jit(solution)/shard_map/pallas_call | solution.py:221
  74.8 0.2 multiply_convert_fusion.2
  75.0 0.4 pad_maximum_fusion
  75.4 1.2 %gather_fusion = bf16[32,8,2,4,128]{4,3,1,2,0:T(4,128)(2,1)S(1)} fusion(bf16[8,2,32,4,128]{4,3,2,0,1:T(4,128)(2,1)S(1)} %pad_maximum_fusion, s32[1024]{0:T(1024)S(1)} %pad_clamp_fusion), kind=kCustom, calls=%fused_computation | custom fusion | bytes 1048704 | tf_op jit(solution)/shard_map/jit(_take)/gather | solution.py:322
  76.6 1.1 %broadcast_select_fusion = bf16[32,8,2,4,128]{4,3,1,2,0:T(4,128)(2,1)} fusion(bf16[32,8,2,4,128]{4,3,1,2,0:T(4,128)(2,1)S(1)} %gather_fusion, pred[32]{0:T(512)(128)(4,1)S(1)} %compare_and_fusion), kind=kLoop, calls=%fused_computation.36 | loop fusion | flops 262144 | bytes 1048608 | tf_op jit(solution)/shard_map/jit(_take)/select_n | solution.py:322
  77.7 4.0 %all-to-all-start = ((bf16[32,8,2,4,128]{4,3,1,2,0:T(4,128)(2,1)}), bf16[32,8,2,4,128]{4,3,1,2,0:T(4,128)(2,1)S(1)}, u32[]{:S(2)}, u32[]{:S(2)}) async-start(bf16[32,8,2,4,128]{4,3,1,2,0:T(4,128)(2,1)} %broadcast_select_fusion), calls=%async_computation | async-start | bytes 1048576 | tf_op jit(solution)/shard_map/all_to_all | solution.py:323
  81.7 0.4 fusion.46
  82.1 0.6 multiply_convert_fusion.3
  82.7 0.4 select_reduce_fusion
  83.1 0.6 fusion.56
  83.7 13.8 %all-to-all-done = bf16[32,8,2,4,128]{4,3,1,2,0:T(4,128)(2,1)S(1)} async-done(((bf16[32,8,2,4,128]{4,3,1,2,0:T(4,128)(2,1)}), bf16[32,8,2,4,128]{4,3,1,2,0:T(4,128)(2,1)S(1)}, u32[]{:S(2)}, u32[]{:S(2)}) %all-to-all-start) | async-done | bytes 524320 | tf_op jit(solution)/shard_map/all_to_all | solution.py:323
  97.5 0.4 fusion.77
  97.9 0.1 fusion.34
  98.0 0.1 fusion.15
  98.2 0.9 reshape.455
  99.1 0.6 fusion.64
  (19 shorter events, 0.2 us)
Async XLA Ops:
  0.6 1.6 %copy-start = (bf16[4,1,2,132992]{3,2,1,0:T(2,128)(2,1)S(1)}, bf16[4,1,2,132992]{3,2,1,0:T(2,128)(2,1)}, u32[]{:S(2)}) copy-start(bf16[4,1,2,132992]{3,2,1,0:T(2,128)(2,1)} %param.4) | copy-start | bytes 6383620
  1.4 2.6 %copy-start.3 = (s32[32]{0:T(128)S(1)}, s32[32]{0:T(128)}, u32[]{:S(2)}) copy-start(s32[32]{0:T(128)} %param.7) | copy-start | bytes 388
  1.4 3.4 %copy-start.2 = (s32[4]{0:T(128)S(1)}, s32[4]{0:T(128)}, u32[]{:S(2)}) copy-start(s32[4]{0:T(128)} %param.5) | copy-start | bytes 52
  1.4 4.0 %slice-start = ((bf16[4,1,2,132992]{3,2,1,0:T(2,128)(2,1)}), bf16[4,1,2,67584]{3,2,1,0:T(2,128)(2,1)S(1)}, s32[]{:S(2)}) async-start(bf16[4,1,2,132992]{3,2,1,0:T(2,128)(2,1)} %param.4), calls=%async_computation.1 | async-start | bytes 2162688 | tf_op jit(solution)/shard_map/slice | solution.py:264
  2.2 4.0 %copy-start.1 = (s32[256]{0:T(256)S(1)}, s32[256]{0:T(256)}, u32[]{:S(2)}) copy-start(s32[256]{0:T(256)} %param.6) | copy-start | bytes 3076
  77.7 19.8 %all-to-all-start = ((bf16[32,8,2,4,128]{4,3,1,2,0:T(4,128)(2,1)}), bf16[32,8,2,4,128]{4,3,1,2,0:T(4,128)(2,1)S(1)}, u32[]{:S(2)}, u32[]{:S(2)}) async-start(bf16[32,8,2,4,128]{4,3,1,2,0:T(4,128)(2,1)} %broadcast_select_fusion), calls=%async_computation | async-start | bytes 1048576 | tf_op jit(solution)/shard_map/all_to_all | solution.py:323
